TPU v7x, 256 devices: a whole 4x4x8 slice. The times are simulated.
256 devices in a mesh: blk: 128 (over x, y, z), ch: 2 (over core).
Axes of the slice: x: 4, y: 4, z: 8, core: 2. Of those that a mesh axis runs over, the one named last changes fastest.
Arguments:
- features: bfloat16 [32768, 128], P('blk'), may hold values from -6 to 6
- out_grad: bfloat16 [32768, 256], P('blk', 'ch'), may hold values from -6 to 6
- weight: bfloat16 [256, 256], P('ch'), may hold values from -0.375 to 0.375
- neighbour_slot: int32 [32768, 20], P('blk'), may hold values from 0 to 2303
- argmax_edge: int32 [32768, 256], P('blk', 'ch'), may hold values from 0 to 19
Outputs:
- feature_grad: float32 [32768, 128], P('blk')
- weight_grad: float32 [256, 256], P('ch')
Inputs may be any that keep to these rules, and one draw needn't show every extreme that they name: `neighbour_slot`: slot s stands for row s mod 256 of the block s // 256 - 4 places away from the point's own block around the cycle.
All inputs are finite; a program needn't handle non-finite values.
Results may differ from a plain program's by a relative error of at most 0.0044.
Values may be sent and summed in bfloat16 or wider, within the bound.
A program may use at most 64 MiB of HBM per device.

v0:
```python
import jax
import jax.numpy as jnp
from jax import lax
from jax.sharding import Mesh
from jax.sharding import PartitionSpec as P

REACH = 4
BLK = ("blk_0", "blk_1", "blk_2")


def shifted(block, axis, distance):
    devices = range(lax.axis_size(axis))
    route = [((i - distance) % len(devices), i) for i in devices]
    return lax.ppermute(block, axis, route)


def split_up(value, dim, count):
    before, after = (value.shape[:dim], value.shape[dim + 1 :])
    return jnp.moveaxis(value.reshape(*before, count, -1, *after), dim, 0)


def summed_on_arrival(value, axis, dim):
    count = lax.axis_size(axis)
    pieces = lax.all_to_all(split_up(value, dim, count), axis, 0, 0, tiled=True)
    return jnp.sum(pieces, axis=0)


def sum_by_axis(value, axes, dim):
    far, near = axes
    pieces = split_up(value, dim, lax.axis_size(far))
    nearer = summed_on_arrival(pieces, near, dim + 1)
    arrived = lax.all_to_all(nearer, far, split_axis=0, concat_axis=0, tiled=True)
    return arrived.sum(axis=0)


def padded_to(lines, count):
    spare = -len(lines) % count
    return jnp.pad(lines, [(0, spare)] + [(0, 0)] * (lines.ndim - 1))


def from_everyone(value, axis):
    copies = jnp.broadcast_to(value, (lax.axis_size(axis), *value.shape))
    return lax.all_to_all(copies, axis, split_axis=0, concat_axis=0, tiled=True)


def laid_out(pieces, dim):
    shape = list(pieces.shape[1:])
    shape[dim] *= pieces.shape[0]
    return jnp.moveaxis(pieces, 0, dim).reshape(shape)


def gather_axes(value, axes, dim):
    far, near = axes
    first = from_everyone(value, far)
    pieces = jnp.swapaxes(from_everyone(first, near), 0, 1)
    return laid_out(pieces.reshape(-1, *value.shape), dim)


def total_of(value, axes):
    lines = value.reshape(-1, value.shape[-1])
    own = sum_by_axis(padded_to(lines, lax.axis_size(axes[0]) * lax.axis_size(axes[1])), axes, 0)
    whole = gather_axes(own, axes, 0)
    return whole[: len(lines)].reshape(value.shape)


def of_everyone(value, axis):
    return from_everyone(value, axis).sum(axis=0)


def silu_slope(pre):
    sig = jax.nn.sigmoid(pre)
    return sig * (1.0 + pre * (1.0 - sig))


def fetch_blocks(piece):
    later = []
    moving = piece
    for turn_count in range(REACH):
        moving = shifted(moving, BLK, -1)
        later.append(moving)
    earlier = []
    moving = piece
    for turn_count in range(REACH):
        moving = shifted(moving, BLK, 1)
        earlier.append(moving)
    return earlier[::-1] + later


def on_device(features, out_grad, weight, neighbour_slot, argmax_edge):
    points = features.shape[0]
    in_width = features.shape[1]
    columns = weight.shape[0]
    neighbours = neighbour_slot.shape[1]
    w_self = weight[:, :in_width]
    w_nbr = weight[:, in_width:]
    w_diff = (w_self.astype(jnp.float32) - w_nbr.astype(jnp.float32)).astype(jnp.bfloat16)
    remote_list = fetch_blocks(features)
    window = jnp.concatenate(remote_list[:REACH] + [features] + remote_list[REACH:], axis=0)
    window_rows = window.shape[0]
    self_term = jnp.dot(features, w_diff.T, preferred_element_type=jnp.float32)
    w_nbr_t = w_nbr.T
    block_rows = min(256, points)
    block_count = points // block_rows
    window_ids = jnp.arange(window_rows, dtype=jnp.int32)
    edge_order = jnp.arange(neighbours, dtype=jnp.int32)

    def point_block(window_acc, inputs):
        self_rows, slot_rows, grad_rows, pick_rows = inputs
        grad_float = grad_rows.astype(jnp.float32)

        def per_edge(carry, edge_index):
            acc_window, edge_total = carry
            slot_col = lax.dynamic_slice_in_dim(slot_rows, edge_index, 1, 1)
            one_hot = (slot_col == window_ids[None, :]).astype(jnp.bfloat16)
            picked = jnp.dot(one_hot, window, preferred_element_type=jnp.float32).astype(
                jnp.bfloat16
            )
            pre = self_rows + jnp.dot(picked, w_nbr_t, preferred_element_type=jnp.float32)
            keep = pick_rows == edge_index
            edge_grad = jnp.where(keep, grad_float * silu_slope(pre), 0.0).astype(jnp.bfloat16)
            edge_total = edge_total + edge_grad.astype(jnp.float32)
            acc_window = acc_window + lax.dot_general(
                one_hot, edge_grad, (((0,), (0,)), ((), ())), preferred_element_type=jnp.float32
            )
            return ((acc_window, edge_total), None)

        start_total = jnp.zeros((self_rows.shape[0], columns), jnp.float32)
        (window_acc, edge_total), _ = lax.scan(per_edge, (window_acc, start_total), edge_order)
        return (window_acc, edge_total.astype(jnp.bfloat16))

    start_window = jnp.zeros((window_rows, columns), jnp.float32)
    gathered_float, grad_sum = lax.scan(
        point_block,
        start_window,
        (
            self_term.reshape(block_count, block_rows, columns),
            neighbour_slot.reshape(block_count, block_rows, neighbours),
            out_grad.reshape(block_count, block_rows, columns),
            argmax_edge.reshape(block_count, block_rows, columns),
        ),
    )
    gathered = gathered_float.astype(jnp.bfloat16)
    grad_sum = grad_sum.reshape(points, columns)
    own_part = lax.dot_general(
        grad_sum, features, (((0,), (0,)), ((), ())), preferred_element_type=jnp.float32
    )
    nbr_total = lax.dot_general(
        gathered, window, (((0,), (0,)), ((), ())), preferred_element_type=jnp.float32
    )
    weight_terms = jnp.concatenate([own_part, nbr_total - own_part], axis=1)
    total_points = points * lax.axis_size(BLK)
    weight_grad = total_of(weight_terms, ("blk_0", ("blk_1", "blk_2"))) * total_points ** (-0.5)
    self_grad = jnp.dot(grad_sum, w_diff, preferred_element_type=jnp.float32)
    pieces = gathered.reshape(2 * REACH + 1, points, columns)
    received = pieces[REACH].astype(jnp.float32)
    for position in range(2 * REACH + 1):
        if position != REACH:
            received = received + shifted(pieces[position], BLK, position - REACH).astype(
                jnp.float32
            )
    local_grad = (
        jnp.dot(
            received,
            w_nbr.astype(jnp.float32),
            precision=lax.Precision.HIGHEST,
            preferred_element_type=jnp.float32,
        )
        + self_grad
    )
    feature_grad = of_everyone(local_grad, "ch")
    return (feature_grad, weight_grad)


def solution(mesh):
    finer = Mesh(mesh.devices.reshape(4, 4, 8, mesh.shape["ch"]), ("blk_0", "blk_1", "blk_2", "ch"))
    return jax.shard_map(
        on_device,
        mesh=finer,
        in_specs=(P(BLK, None), P(BLK, "ch"), P("ch", None), P(BLK, None), P(BLK, "ch")),
        out_specs=(P(BLK, None), P("ch", None)),
        check_vma=False,
    )
```

profile of v0, /device:TPU:1, one launch (start us, length us, event | category | flops | bytes accessed | tf_op | source)
XLA Modules:
  0.0 235.4 jit_solution(13545924017322563125)
XLA Ops:
  0.7 2.5 %collective-permute-start = (bf16[256,128]{1,0:T(8,128)(2,1)}, bf16[256,128]{1,0:T(8,128)(2,1)S(1)}, u32[]{:S(2)}, u32[]{:S(2)}) collective-permute-start(bf16[256,128]{1,0:T(8,128)(2,1)} %param.7), channel_id=1, source_target_pairs={{254,0},{0,2},{2,4},{4,6},{6,8},{8,10},{10,12},{12,14},{14,16},{16... | collective-permute-start | bytes 196616 | tf_op jit(solution)/shard_map/ppermute | solution.py:14
  3.2 8.7 %collective-permute-start.4 = (bf16[256,128]{1,0:T(8,128)(2,1)}, bf16[256,128]{1,0:T(8,128)(2,1)S(1)}, u32[]{:S(2)}, u32[]{:S(2)}) collective-permute-start(bf16[256,128]{1,0:T(8,128)(2,1)} %param.7), channel_id=1, source_target_pairs={{2,0},{4,2},{6,4},{8,6},{10,8},{12,10},{14,12},{16,14},{18,16},{20... | collective-permute-start | bytes 196616 | tf_op jit(solution)/shard_map/ppermute | solution.py:14
  11.9 1.8 collective-permute-done
  13.6 7.0 %collective-permute-start.5 = (bf16[256,128]{1,0:T(8,128)(2,1)S(1)}, bf16[256,128]{1,0:T(8,128)(2,1)S(1)}, u32[]{:S(2)}, u32[]{:S(2)}) collective-permute-start(bf16[256,128]{1,0:T(8,128)(2,1)S(1)} %collective-permute-done.4), channel_id=1, source_target_pairs={{2,0},{4,2},{6,4},{8,6},{10,8},{12,10},{14,12},{16,14},{18,16},{20... | collective-permute-start | bytes 196616 | tf_op jit(solution)/shard_map/ppermute | solution.py:14
  20.6 1.6 collective-permute-done.1
  23.2 7.0 %collective-permute-start.6 = (bf16[256,128]{1,0:T(8,128)(2,1)S(1)}, bf16[256,128]{1,0:T(8,128)(2,1)S(1)}, u32[]{:S(2)}, u32[]{:S(2)}) collective-permute-start(bf16[256,128]{1,0:T(8,128)(2,1)S(1)} %collective-permute-done.5), channel_id=1, source_target_pairs={{2,0},{4,2},{6,4},{8,6},{10,8},{12,10},{14,12},{16,14},{18,16},{20... | collective-permute-start | bytes 196616 | tf_op jit(solution)/shard_map/ppermute | solution.py:14
  32.7 7.0 %collective-permute-start.7 = (bf16[256,128]{1,0:T(8,128)(2,1)S(1)}, bf16[256,128]{1,0:T(8,128)(2,1)S(1)}, u32[]{:S(2)}, u32[]{:S(2)}) collective-permute-start(bf16[256,128]{1,0:T(8,128)(2,1)S(1)} %collective-permute-done.6), channel_id=1, source_target_pairs={{2,0},{4,2},{6,4},{8,6},{10,8},{12,10},{14,12},{16,14},{18,16},{20... | collective-permute-start | bytes 196616 | tf_op jit(solution)/shard_map/ppermute | solution.py:14
  41.1 117.4 %while.22 = (s32[]{:T(128)}, f32[2304,128]{1,0:T(8,128)S(1)}, f32[256,128]{1,0:T(8,128)S(1)}, s32[20]{0:T(128)S(1)}, s32[256,20]{0,1:T(8,128)}, /*index=5*/s32[2...) while((s32[]{:T(128)}, f32[2304,128]{1,0:T(8,128)S(1)}, ...), condition=%wide.region_1.2_spmd.clone, body=%wide.region_0.1_spmd.clone.sunk | while | flops 312672256 | bytes 3772614 | solution.py:128
  44.3 1.3 select_add_fusion.2
  50.2 1.3 select_add_fusion.2
  56.1 1.3 select_add_fusion.2
  61.9 1.3 select_add_fusion.2
  67.8 1.3 select_add_fusion.2
  150.0 1.3 select_add_fusion.2
  160.0 3.9 %all-to-all-start.1 = ((f32[32,4,1,256]{3,1,2,0:T(4,128)}), f32[32,4,1,256]{3,1,2,0:T(4,128)S(1)}, u32[]{:S(2)}, u32[]{:S(2)}) async-start(f32[32,4,1,256]{3,1,2,0:T(4,128)} %copy.29), calls=%async_computation.1 | async-start | bytes 262144 | tf_op jit(solution)/shard_map/all_to_all | solution.py:24
  163.9 12.4 %collective-permute-start.8 = (bf16[256,128]{1,0:T(8,128)(2,1)S(1)}, bf16[256,128]{1,0:T(8,128)(2,1)S(1)}, u32[]{:S(2)}, u32[]{:S(2)}) collective-permute-start(bf16[256,128]{1,0:T(8,128)(2,1)S(1)} %get-tuple-element.202), channel_id=1, source_target_pairs={{8,0},{10,2},{12,4},{14,6},{16,8},{18,10},{20,12},{22,14},{24,16},... | collective-permute-start | bytes 196616 | tf_op jit(solution)/shard_map/ppermute | solution.py:14
  177.6 5.6 %all-to-all-start.2 = ((f32[4,1,256]{2,1,0:T(1,128)}), f32[4,1,256]{2,1,0:T(1,128)S(1)}, u32[]{:S(2)}, u32[]{:S(2)}) async-start(f32[4,1,256]{2,1,0:T(1,128)} %reduce_sum.31), calls=%async_computation.2 | async-start | bytes 8192 | tf_op jit(solution)/shard_map/all_to_all | solution.py:32
  183.2 7.8 %collective-permute-start.11 = (bf16[256,128]{1,0:T(8,128)(2,1)S(1)}, bf16[256,128]{1,0:T(8,128)(2,1)S(1)}, u32[]{:S(2)}, u32[]{:S(2)}) collective-permute-start(bf16[256,128]{1,0:T(8,128)(2,1)S(1)} %get-tuple-element.207), channel_id=1, source_target_pairs={{2,0},{4,2},{6,4},{8,6},{10,8},{12,10},{14,12},{16,14},{18,16},{20... | collective-permute-start | bytes 196616 | tf_op jit(solution)/shard_map/ppermute | solution.py:14
  192.0 2.7 %collective-permute-start.9 = (bf16[256,128]{1,0:T(8,128)(2,1)S(1)}, bf16[256,128]{1,0:T(8,128)(2,1)S(1)}, u32[]{:S(2)}, u32[]{:S(2)}) collective-permute-start(bf16[256,128]{1,0:T(8,128)(2,1)S(1)} %get-tuple-element.209), channel_id=1, source_target_pairs={{6,0},{8,2},{10,4},{12,6},{14,8},{16,10},{18,12},{20,14},{22,16},{... | collective-permute-start | bytes 196616 | tf_op jit(solution)/shard_map/ppermute | solution.py:14
  195.5 3.2 %all-to-all-start.3 = ((f32[4,1,256]{2,1,0:T(1,128)}), f32[4,1,256]{2,1,0:T(1,128)S(1)}, u32[]{:S(2)}, u32[]{:S(2)}) async-start(f32[4,1,256]{2,1,0:T(1,128)} %broadcast_in_dim.23), calls=%async_computation.3 | async-start | bytes 8192 | tf_op jit(solution)/shard_map/all_to_all | solution.py:43
  199.1 3.8 %all-to-all-done.3 = f32[4,1,256]{2,1,0:T(1,128)S(1)} async-done(((f32[4,1,256]{2,1,0:T(1,128)}), f32[4,1,256]{2,1,0:T(1,128)S(1)}, u32[]{:S(2)}, u32[]{:S(2)}) %all-to-all-start.3) | async-done | bytes 4128 | tf_op jit(solution)/shard_map/all_to_all | solution.py:43
  203.6 12.9 %all-to-all-start = ((f32[2,256,128]{2,1,0:T(8,128)}), f32[2,256,128]{2,1,0:T(8,128)S(1)}, u32[]{:S(2)}, u32[]{:S(2)}) async-start(f32[2,256,128]{2,1,0:T(8,128)} %broadcast_in_dim.22), calls=%async_computation | async-start | bytes 524288 | tf_op jit(solution)/shard_map/all_to_all | solution.py:43
  218.4 7.1 %all-to-all-start.4 = ((f32[32,4,1,256]{3,1,2,0:T(4,128)}), f32[32,4,1,256]{3,1,2,0:T(4,128)S(1)}, u32[]{:S(2)}, u32[]{:S(2)}) async-start(f32[32,4,1,256]{3,1,2,0:T(4,128)} %broadcast_in_dim.24), calls=%async_computation.4 | async-start | bytes 262144 | tf_op jit(solution)/shard_map/all_to_all | solution.py:43
  226.2 8.5 %all-to-all-done.4 = f32[32,4,1,256]{3,1,2,0:T(4,128)S(1)} async-done(((f32[32,4,1,256]{3,1,2,0:T(4,128)}), f32[32,4,1,256]{3,1,2,0:T(4,128)S(1)}, u32[]{:S(2)}, u32[]{:S(2)}) %all-to-all-start.4) | async-done | bytes 131104 | tf_op jit(solution)/shard_map/all_to_all | solution.py:43
  (141 shorter events, 83.5 us)
Async XLA Ops:
  0.6 39.2 %copy-start = (bf16[256,128]{1,0:T(8,128)(2,1)S(1)}, bf16[256,128]{1,0:T(8,128)(2,1)}, u32[]{:S(2)}) copy-start(bf16[256,128]{1,0:T(8,128)(2,1)} %param.7) | copy-start | bytes 196612
  0.6 40.4 %copy-start.2 = (s32[256,128]{1,0:T(8,128)S(1)}, s32[256,128]{1,0:T(8,128)}, u32[]{:S(2)}) copy-start(s32[256,128]{1,0:T(8,128)} %param.11) | copy-start | bytes 393220
  0.7 13.0 %collective-permute-start = (bf16[256,128]{1,0:T(8,128)(2,1)}, bf16[256,128]{1,0:T(8,128)(2,1)S(1)}, u32[]{:S(2)}, u32[]{:S(2)}) collective-permute-start(bf16[256,128]{1,0:T(8,128)(2,1)} %param.7), channel_id=1, source_target_pairs={{254,0},{0,2},{2,4},{4,6},{6,8},{8,10},{10,12},{12,14},{14,16},{16... | collective-permute-start | bytes 196616 | tf_op jit(solution)/shard_map/ppermute | solution.py:14
  3.2 10.5 %collective-permute-start.4 = (bf16[256,128]{1,0:T(8,128)(2,1)}, bf16[256,128]{1,0:T(8,128)(2,1)S(1)}, u32[]{:S(2)}, u32[]{:S(2)}) collective-permute-start(bf16[256,128]{1,0:T(8,128)(2,1)} %param.7), channel_id=1, source_target_pairs={{2,0},{4,2},{6,4},{8,6},{10,8},{12,10},{14,12},{16,14},{18,16},{20... | collective-permute-start | bytes 196616 | tf_op jit(solution)/shard_map/ppermute | solution.py:14
  13.6 8.5 %collective-permute-start.1 = (bf16[256,128]{1,0:T(8,128)(2,1)S(1)}, bf16[256,128]{1,0:T(8,128)(2,1)S(1)}, u32[]{:S(2)}, u32[]{:S(2)}) collective-permute-start(bf16[256,128]{1,0:T(8,128)(2,1)S(1)} %collective-permute-done), channel_id=1, source_target_pairs={{254,0},{0,2},{2,4},{4,6},{6,8},{8,10},{10,12},{12,14},{14,16},{16... | collective-permute-start | bytes 196616 | tf_op jit(solution)/shard_map/ppermute | solution.py:14
  13.6 9.6 %collective-permute-start.5 = (bf16[256,128]{1,0:T(8,128)(2,1)S(1)}, bf16[256,128]{1,0:T(8,128)(2,1)S(1)}, u32[]{:S(2)}, u32[]{:S(2)}) collective-permute-start(bf16[256,128]{1,0:T(8,128)(2,1)S(1)} %collective-permute-done.4), channel_id=1, source_target_pairs={{2,0},{4,2},{6,4},{8,6},{10,8},{12,10},{14,12},{16,14},{18,16},{20... | collective-permute-start | bytes 196616 | tf_op jit(solution)/shard_map/ppermute | solution.py:14
  22.2 8.5 %collective-permute-start.2 = (bf16[256,128]{1,0:T(8,128)(2,1)S(1)}, bf16[256,128]{1,0:T(8,128)(2,1)S(1)}, u32[]{:S(2)}, u32[]{:S(2)}) collective-permute-start(bf16[256,128]{1,0:T(8,128)(2,1)S(1)} %collective-permute-done.1), channel_id=1, source_target_pairs={{254,0},{0,2},{2,4},{4,6},{6,8},{8,10},{10,12},{12,14},{14,16},{16... | collective-permute-start | bytes 196616 | tf_op jit(solution)/shard_map/ppermute | solution.py:14
  23.2 9.5 %collective-permute-start.6 = (bf16[256,128]{1,0:T(8,128)(2,1)S(1)}, bf16[256,128]{1,0:T(8,128)(2,1)S(1)}, u32[]{:S(2)}, u32[]{:S(2)}) collective-permute-start(bf16[256,128]{1,0:T(8,128)(2,1)S(1)} %collective-permute-done.5), channel_id=1, source_target_pairs={{2,0},{4,2},{6,4},{8,6},{10,8},{12,10},{14,12},{16,14},{18,16},{20... | collective-permute-start | bytes 196616 | tf_op jit(solution)/shard_map/ppermute | solution.py:14
  30.7 9.0 %collective-permute-start.3 = (bf16[256,128]{1,0:T(8,128)(2,1)S(1)}, bf16[256,128]{1,0:T(8,128)(2,1)S(1)}, u32[]{:S(2)}, u32[]{:S(2)}) collective-permute-start(bf16[256,128]{1,0:T(8,128)(2,1)S(1)} %collective-permute-done.2), channel_id=1, source_target_pairs={{254,0},{0,2},{2,4},{4,6},{6,8},{8,10},{10,12},{12,14},{14,16},{16... | collective-permute-start | bytes 196616 | tf_op jit(solution)/shard_map/ppermute | solution.py:14
  32.7 8.3 %collective-permute-start.7 = (bf16[256,128]{1,0:T(8,128)(2,1)S(1)}, bf16[256,128]{1,0:T(8,128)(2,1)S(1)}, u32[]{:S(2)}, u32[]{:S(2)}) collective-permute-start(bf16[256,128]{1,0:T(8,128)(2,1)S(1)} %collective-permute-done.6), channel_id=1, source_target_pairs={{2,0},{4,2},{6,4},{8,6},{10,8},{12,10},{14,12},{16,14},{18,16},{20... | collective-permute-start | bytes 196616 | tf_op jit(solution)/shard_map/ppermute | solution.py:14
  159.2 39.7 %copy-start.1 = (bf16[128,256]{1,0:T(8,128)(2,1)S(1)}, bf16[128,256]{1,0:T(8,128)(2,1)}, u32[]{:S(2)}) copy-start(bf16[128,256]{1,0:T(8,128)(2,1)} %param.9) | copy-start | bytes 196612
  160.0 16.9 %all-to-all-start.1 = ((f32[32,4,1,256]{3,1,2,0:T(4,128)}), f32[32,4,1,256]{3,1,2,0:T(4,128)S(1)}, u32[]{:S(2)}, u32[]{:S(2)}) async-start(f32[32,4,1,256]{3,1,2,0:T(4,128)} %copy.29), calls=%async_computation.1 | async-start | bytes 262144 | tf_op jit(solution)/shard_map/all_to_all | solution.py:24
  163.9 19.3 %collective-permute-start.8 = (bf16[256,128]{1,0:T(8,128)(2,1)S(1)}, bf16[256,128]{1,0:T(8,128)(2,1)S(1)}, u32[]{:S(2)}, u32[]{:S(2)}) collective-permute-start(bf16[256,128]{1,0:T(8,128)(2,1)S(1)} %get-tuple-element.202), channel_id=1, source_target_pairs={{8,0},{10,2},{12,4},{14,6},{16,8},{18,10},{20,12},{22,14},{24,16},... | collective-permute-start | bytes 196616 | tf_op jit(solution)/shard_map/ppermute | solution.py:14
  176.3 14.7 %collective-permute-start.15 = (bf16[256,128]{1,0:T(8,128)(2,1)S(1)}, bf16[256,128]{1,0:T(8,128)(2,1)S(1)}, u32[]{:S(2)}, u32[]{:S(2)}) collective-permute-start(bf16[256,128]{1,0:T(8,128)(2,1)S(1)} %get-tuple-element.203), channel_id=1, source_target_pairs={{248,0},{250,2},{252,4},{254,6},{0,8},{2,10},{4,12},{6,14},{8,16},... | collective-permute-start | bytes 196616 | tf_op jit(solution)/shard_map/ppermute | solution.py:14
  176.3 15.6 %collective-permute-start.14 = (bf16[256,128]{1,0:T(8,128)(2,1)S(1)}, bf16[256,128]{1,0:T(8,128)(2,1)S(1)}, u32[]{:S(2)}, u32[]{:S(2)}) collective-permute-start(bf16[256,128]{1,0:T(8,128)(2,1)S(1)} %get-tuple-element.204), channel_id=1, source_target_pairs={{250,0},{252,2},{254,4},{0,6},{2,8},{4,10},{6,12},{8,14},{10,16},{... | collective-permute-start | bytes 196616 | tf_op jit(solution)/shard_map/ppermute | solution.py:14
  176.6 22.1 %collective-permute-start.13 = (bf16[256,128]{1,0:T(8,128)(2,1)S(1)}, bf16[256,128]{1,0:T(8,128)(2,1)S(1)}, u32[]{:S(2)}, u32[]{:S(2)}) collective-permute-start(bf16[256,128]{1,0:T(8,128)(2,1)S(1)} %get-tuple-element.205), channel_id=1, source_target_pairs={{252,0},{254,2},{0,4},{2,6},{4,8},{6,10},{8,12},{10,14},{12,16},{1... | collective-permute-start | bytes 196616 | tf_op jit(solution)/shard_map/ppermute | solution.py:14
  176.7 22.1 %collective-permute-start.12 = (bf16[256,128]{1,0:T(8,128)(2,1)S(1)}, bf16[256,128]{1,0:T(8,128)(2,1)S(1)}, u32[]{:S(2)}, u32[]{:S(2)}) collective-permute-start(bf16[256,128]{1,0:T(8,128)(2,1)S(1)} %get-tuple-element.206), channel_id=1, source_target_pairs={{254,0},{0,2},{2,4},{4,6},{6,8},{8,10},{10,12},{12,14},{14,16},{16... | collective-permute-start | bytes 196616 | tf_op jit(solution)/shard_map/ppermute | solution.py:14
  177.6 17.3 %all-to-all-start.2 = ((f32[4,1,256]{2,1,0:T(1,128)}), f32[4,1,256]{2,1,0:T(1,128)S(1)}, u32[]{:S(2)}, u32[]{:S(2)}) async-start(f32[4,1,256]{2,1,0:T(1,128)} %reduce_sum.31), calls=%async_computation.2 | async-start | bytes 8192 | tf_op jit(solution)/shard_map/all_to_all | solution.py:32
  183.2 15.6 %collective-permute-start.11 = (bf16[256,128]{1,0:T(8,128)(2,1)S(1)}, bf16[256,128]{1,0:T(8,128)(2,1)S(1)}, u32[]{:S(2)}, u32[]{:S(2)}) collective-permute-start(bf16[256,128]{1,0:T(8,128)(2,1)S(1)} %get-tuple-element.207), channel_id=1, source_target_pairs={{2,0},{4,2},{6,4},{8,6},{10,8},{12,10},{14,12},{16,14},{18,16},{20... | collective-permute-start | bytes 196616 | tf_op jit(solution)/shard_map/ppermute | solution.py:14
  191.0 7.8 %collective-permute-start.10 = (bf16[256,128]{1,0:T(8,128)(2,1)S(1)}, bf16[256,128]{1,0:T(8,128)(2,1)S(1)}, u32[]{:S(2)}, u32[]{:S(2)}) collective-permute-start(bf16[256,128]{1,0:T(8,128)(2,1)S(1)} %get-tuple-element.208), channel_id=1, source_target_pairs={{4,0},{6,2},{8,4},{10,6},{12,8},{14,10},{16,12},{18,14},{20,16},{2... | collective-permute-start | bytes 196616 | tf_op jit(solution)/shard_map/ppermute | solution.py:14
  192.0 6.8 %collective-permute-start.9 = (bf16[256,128]{1,0:T(8,128)(2,1)S(1)}, bf16[256,128]{1,0:T(8,128)(2,1)S(1)}, u32[]{:S(2)}, u32[]{:S(2)}) collective-permute-start(bf16[256,128]{1,0:T(8,128)(2,1)S(1)} %get-tuple-element.209), channel_id=1, source_target_pairs={{6,0},{8,2},{10,4},{12,6},{14,8},{16,10},{18,12},{20,14},{22,16},{... | collective-permute-start | bytes 196616 | tf_op jit(solution)/shard_map/ppermute | solution.py:14
  195.5 7.4 %all-to-all-start.3 = ((f32[4,1,256]{2,1,0:T(1,128)}), f32[4,1,256]{2,1,0:T(1,128)S(1)}, u32[]{:S(2)}, u32[]{:S(2)}) async-start(f32[4,1,256]{2,1,0:T(1,128)} %broadcast_in_dim.23), calls=%async_computation.3 | async-start | bytes 8192 | tf_op jit(solution)/shard_map/all_to_all | solution.py:43
  203.6 14.1 %all-to-all-start = ((f32[2,256,128]{2,1,0:T(8,128)}), f32[2,256,128]{2,1,0:T(8,128)S(1)}, u32[]{:S(2)}, u32[]{:S(2)}) async-start(f32[2,256,128]{2,1,0:T(8,128)} %broadcast_in_dim.22), calls=%async_computation | async-start | bytes 524288 | tf_op jit(solution)/shard_map/all_to_all | solution.py:43
  218.4 16.3 %all-to-all-start.4 = ((f32[32,4,1,256]{3,1,2,0:T(4,128)}), f32[32,4,1,256]{3,1,2,0:T(4,128)S(1)}, u32[]{:S(2)}, u32[]{:S(2)}) async-start(f32[32,4,1,256]{3,1,2,0:T(4,128)} %broadcast_in_dim.24), calls=%async_computation.4 | async-start | bytes 262144 | tf_op jit(solution)/shard_map/all_to_all | solution.py:43
where the time goes:
time: 237 us; the launch traced here: 235 us
  starting transfers between devices  89.4 us (38%)
  matrix products  54 us (23%)
  loops' own time  39.5 us (17%)
  local copies, waits for them, and re-layouts  30.6 us (13%)
  waiting for transfers between devices  18.6 us (8%)
    ppermute x16, starting transfers between devices, shifted(): return lax.ppermute(block, axis, route)  56.6 us
    another operation x1, loops' own time, point_block(): lax.scan(per_edge, (window_acc, start_total), edge_order)  39.5 us
    dot_general x20, matrix products, per_edge(): jnp.dot(picked, w_nbr_t, preferred_element_type=jnp.float32)  26.6 us
    dot_general x20, matrix products, per_edge(): lax.dot_general(one_hot, edge_grad, (((0,), (0,)), ((), ())), preferred_e...  25.4 us
    all_to_all x3, starting transfers between devices, from_everyone(): return lax.all_to_all(copies, axis, split_axis=0, concat_axis=0, tiled=True)  23.3 us
    dynamic_slice x20, local copies, waits for them, and re-layouts, per_edge(): slot_col = lax.dynamic_slice_in_dim(slot_rows, edge_index, 1, 1)  14.1 us
    all_to_all x3, waiting for transfers between devices, from_everyone(): return lax.all_to_all(copies, axis, split_axis=0, concat_axis=0, tiled=True)  13.5 us
    dynamic_slice x20, local copies, waits for them, and re-layouts, point_block(): lax.scan(per_edge, (window_acc, start_total), edge_order)  11.8 us
  transfers between devices with their start and end apart: 21, of which 7 were waited for; matrix products, arithmetic and copies ran while one was open for 2% of the time, Pallas kernels for 0%

commit v1 on v0

v1 whole, which is shorter than its diff:
```python
import jax
import jax.numpy as jnp
from jax import lax
from jax.experimental import pallas as pl
from jax.experimental.pallas import tpu as pltpu
from jax.sharding import PartitionSpec as P

REACH = 4
SPAN = 2 * REACH + 1
NB = 128
PTS = 256
HALF = 128
CIN = 128
KNN = 20
MESH = pl.DeviceIdType.MESH
F32, BF16, I32 = jnp.float32, jnp.bfloat16, jnp.int32
NT = (((1,), (1,)), ((), ()))
TN = (((0,), (0,)), ((), ()))
FAR = (4, -4, 3, -3, 2, -2, 1, -1)
XY = sorted(
    [(dx, dy) for dx in range(4) for dy in range(4) if dx or dy],
    key=lambda t: -(min(t[0], 4 - t[0]) + min(t[1], 4 - t[1])),
)
ZO = (4, 3, 5, 2, 6, 1, 7)


def silu_slope(pre):
    sig = jax.nn.sigmoid(pre)
    return sig * (1.0 + pre * (1.0 - sig))


def kernel(
    f_hbm, g_hbm, w_hbm, s_hbm, a_hbm, fg_hbm, wg_hbm,
    win, gv, wv, sv, av, spad, s_t, low_t, grp_t, onehot, edges, pre, acc,
    part_out, part_in, mine, summed, got, fgv, wgv, rs_in, z_in, piece, wgo,
    in_sem, far_s, far_r, half_s, half_r, pp_s, pp_r, c_s, c_r,
    a1s, a1r, a2s, a2r, a3s, a3r, fo_s, fo_r, out_sem,
):
    b = lax.axis_index("blk")
    c = lax.axis_index("ch")
    partner = (b, 1 - c)
    line, z = b // 8, b % 8
    x, y = line // 4, line % 4
    far = [(lax.rem(b + k + NB, NB), c) for k in FAR]
    plane_at = [lax.rem(x + dx, 4) * 4 + lax.rem(y + dy, 4) for dx, dy in XY]
    plane = [(q * 8 + z, c) for q in plane_at]
    zline = [(line * 8 + lax.rem(z + dz, 8), c) for dz in ZO]

    bar = pltpu.get_barrier_semaphore()
    peers = far + [partner] + zline + plane
    for d in peers:
        pl.semaphore_signal(bar, inc=1, device_id=d, device_id_type=MESH)
    loads = [
        pltpu.make_async_copy(f_hbm, win.at[REACH], in_sem.at[0]),
        pltpu.make_async_copy(s_hbm, sv, in_sem.at[1]),
        pltpu.make_async_copy(a_hbm, av, in_sem.at[2]),
        pltpu.make_async_copy(w_hbm, wv, in_sem.at[3]),
        pltpu.make_async_copy(g_hbm, gv, in_sem.at[4]),
    ]
    for cp in loads:
        cp.start()
    loads[0].wait()
    pl.semaphore_wait(bar, len(peers))

    my_rows = pl.ds(pl.multiple_of(c * HALF, HALF), HALF)
    its_rows = pl.ds(pl.multiple_of((1 - c) * HALF, HALF), HALF)

    def rcopy(src, dst, ss, rs, dev):
        return pltpu.make_async_remote_copy(
            src_ref=src, dst_ref=dst, send_sem=ss, recv_sem=rs, device_id=dev, device_id_type=MESH
        )

    far_cp = []
    for k, d in zip(FAR, far):
        w = REACH - k
        cp = rcopy(win.at[REACH, my_rows], win.at[w, my_rows], far_s.at[w], far_r.at[w], d)
        cp.start()
        far_cp.append(cp)

    for cp in loads[1:]:
        cp.wait()
    spad[...] = jnp.zeros_like(spad)
    spad[:, :KNN] = sv[...]
    idx = jnp.take_along_axis(spad[...], av[...], axis=1, mode="promise_in_bounds")
    idx_t = idx.T
    low_t[...] = idx_t & 127
    grp_t[...] = idx_t >> 7
    s_t[...] = spad[...].T
    w_nbr = wv[:, CIN:]
    w_diff = (wv[:, :CIN].astype(F32) - w_nbr.astype(F32)).astype(BF16)
    row_ids = lax.broadcasted_iota(I32, (HALF, PTS), 0).astype(F32).astype(BF16)

    @pl.loop(0, KNN)
    def _(k):
        row = s_t[pl.ds(k, 1), :]
        low = (row & 127).astype(F32)
        blk = row >> 8
        cols = pl.ds(pl.multiple_of(k * PTS, PTS), PTS)
        for w in range(SPAN):
            key = jnp.broadcast_to(jnp.where(blk == w, low, -1.0), (HALF, PTS)).astype(BF16)
            onehot[w * HALF : (w + 1) * HALF, cols] = jnp.where(row_ids == key, 1.0, 0.0).astype(BF16)

    pre[...] = lax.dot_general(w_diff, win[REACH], NT, preferred_element_type=F32)

    def pick(w):
        vals = lax.dot_general(w_nbr, win[w], NT, preferred_element_type=F32)
        for h in range(2):
            cols = slice(h * HALF, (h + 1) * HALF)
            low, grp, p = low_t[:, cols], grp_t[:, cols], pre[:, cols]
            for g in range(2):
                table = vals[:, g * HALF : (g + 1) * HALF]
                hit = jnp.take_along_axis(table, low, axis=1, mode="promise_in_bounds")
                p = jnp.where(grp == 2 * w + g, p + hit, p)
            pre[:, cols] = p

    pick(REACH)
    half_cp = {}
    last = None
    for k in FAR + (None,):
        if k is not None:
            w = REACH - k
            rcopy(win.at[w, my_rows], win.at[w, my_rows], far_s.at[w], far_r.at[w], partner).wait_recv()
            half_cp[w] = rcopy(win.at[w, my_rows], win.at[w, my_rows], half_s.at[w], half_r.at[w], partner)
            half_cp[w].start()
        if last is not None:
            rcopy(win.at[last, my_rows], win.at[last, its_rows], half_s.at[last], half_r.at[last], partner).wait_recv()
            pick(last)
        last = None if k is None else w

    edge = (gv[...].astype(F32) * silu_slope(pre[...].T)).astype(BF16)
    upper = (idx >> 7) & 1
    ef, af = edge.astype(F32), av[...].astype(F32)
    e2 = jnp.concatenate([jnp.where(upper == 0, ef, 0.0), jnp.where(upper == 1, ef, 0.0)], axis=1).astype(BF16)
    a2 = jnp.concatenate([jnp.where(upper == 0, af, -1.0), jnp.where(upper == 1, af, -1.0)], axis=1).astype(BF16)
    for k in range(KNN):
        edges[k * PTS : (k + 1) * PTS, :] = jnp.where(a2 == jnp.asarray(k, BF16), e2, jnp.zeros_like(e2))
    own_part = lax.dot_general(edge, win[REACH], TN, preferred_element_type=F32)
    nbr = jnp.zeros((HALF, CIN), F32)
    part_cp = {}
    for group in ((0, 1, 2), (6, 7, 8), (3, 4, 5)):
        rows = slice(group[0] * HALF, (group[-1] + 1) * HALF)
        acc[rows, :] = jnp.dot(onehot[rows, :], edges[...], preferred_element_type=F32)
        for w in group:
            ga = acc[w * HALF : (w + 1) * HALF, :].astype(BF16)
            ga = jnp.concatenate([ga[:, :HALF], ga[:, HALF:]], axis=0)
            con = jnp.dot(ga, w_nbr, preferred_element_type=F32)
            if w == REACH:
                con = con + jnp.dot(edge, w_diff, preferred_element_type=F32)
            nbr = nbr + lax.dot_general(ga, win[w], TN, preferred_element_type=F32)
            lo, hi = con[:HALF], con[HALF:]
            mine[w] = jnp.where(c == 0, lo, hi)
            part_out[w] = jnp.where(c == 0, hi, lo).astype(BF16)
            part_cp[w] = rcopy(part_out.at[w], part_in.at[w], pp_s.at[w], pp_r.at[w], partner)
            part_cp[w].start()
    wgv[:, :CIN] = own_part
    wgv[:, CIN:] = nbr - own_part

    a1 = []
    for j, (q, d) in enumerate(zip(plane_at, plane)):
        cp = rcopy(wgv.at[pl.ds(pl.multiple_of(q * 8, 8), 8)], rs_in.at[j], a1s.at[j], a1r.at[j], d)
        cp.start()
        a1.append(cp)

    c_cp = []
    for w in (0, 1, 2, 6, 7, 8, 3, 5):
        part_cp[w].wait_recv()
        summed[w] = (mine[w] + part_in[w].astype(F32)).astype(BF16)
        cp = rcopy(summed.at[w], got.at[8 - w], c_s.at[w], c_r.at[8 - w], (lax.rem(b + w - REACH + NB, NB), c))
        cp.start()
        c_cp.append((w, cp))
    part_cp[REACH].wait_recv()
    total = mine[REACH] + part_in[REACH].astype(F32)

    my_piece = pl.ds(pl.multiple_of(line * 8, 8), 8)
    for cp in a1:
        cp.wait_recv()
    piece[0] = wgv[my_piece, :] + jnp.sum(rs_in[...], axis=0)
    a2c = []
    for j, d in enumerate(zline):
        cp = rcopy(piece.at[0], z_in.at[j], a2s.at[j], a2r.at[j], d)
        cp.start()
        a2c.append(cp)
    for cp in a2c:
        cp.wait_recv()
    piece[1] = (piece[0] + jnp.sum(z_in[...], axis=0)) * (NB * PTS) ** -0.5
    a3c = []
    for j, d in enumerate(plane):
        cp = rcopy(piece.at[1], wgo.at[my_piece], a3s.at[j], a3r.at[j], d)
        cp.start()
        a3c.append(cp)
    wgo[my_piece, :] = piece[1]

    for w, cp in c_cp:
        rcopy(summed.at[w], got.at[w], c_s.at[w], c_r.at[w], partner).wait_recv()
        total = total + got[w].astype(F32)
    fgv[my_rows, :] = total
    fo = rcopy(fgv.at[my_rows], fgv.at[my_rows], fo_s, fo_r, partner)
    fo.start()

    for cp in a3c:
        cp.wait_recv()
    out_wg = pltpu.make_async_copy(wgo, wg_hbm, out_sem.at[0])
    out_wg.start()
    rcopy(fgv.at[my_rows], fgv.at[its_rows], fo_s, fo_r, partner).wait_recv()
    out_fg = pltpu.make_async_copy(fgv, fg_hbm, out_sem.at[1])
    out_fg.start()
    for cp in far_cp + list(half_cp.values()) + list(part_cp.values()) + [cp for _, cp in c_cp] + a1 + a2c + a3c + [fo]:
        cp.wait_send()
    out_wg.wait()
    out_fg.wait()


def on_device(features, out_grad, weight, neighbour_slot, argmax_edge):
    v = pltpu.VMEM
    dma = pltpu.SemaphoreType.DMA
    return pl.pallas_call(
        kernel,
        out_shape=(jax.ShapeDtypeStruct((PTS, CIN), F32), jax.ShapeDtypeStruct((HALF, 2 * CIN), F32)),
        in_specs=[pl.BlockSpec(memory_space=pl.ANY)] * 5,
        out_specs=[pl.BlockSpec(memory_space=pl.ANY)] * 2,
        scratch_shapes=[
            v((SPAN, PTS, CIN), BF16), v((PTS, HALF), BF16), v((HALF, 2 * CIN), BF16), v((PTS, KNN), I32),
            v((PTS, HALF), I32), v((PTS, 128), I32), v((128, PTS), I32), v((HALF, PTS), I32), v((HALF, PTS), I32),
            v((SPAN * HALF, KNN * PTS), BF16), v((KNN * PTS, 2 * HALF), BF16), v((HALF, PTS), F32),
            v((SPAN * HALF, 2 * HALF), F32),
            v((SPAN, HALF, CIN), BF16), v((SPAN, HALF, CIN), BF16), v((SPAN, HALF, CIN), F32),
            v((SPAN, HALF, CIN), BF16), v((SPAN, HALF, CIN), BF16), v((PTS, CIN), F32), v((HALF, 2 * CIN), F32),
            v((15, 8, 2 * CIN), F32), v((7, 8, 2 * CIN), F32), v((2, 8, 2 * CIN), F32), v((HALF, 2 * CIN), F32),
            dma((5,)), dma((SPAN,)), dma((SPAN,)), dma((SPAN,)), dma((SPAN,)), dma((SPAN,)), dma((SPAN,)),
            dma((SPAN,)), dma((SPAN,)), dma((15,)), dma((15,)), dma((7,)), dma((7,)), dma((15,)), dma((15,)),
            dma, dma, dma((2,)),
        ],
        compiler_params=pltpu.CompilerParams(
            collective_id=0, has_side_effects=True, vmem_limit_bytes=56 * 2**20
        ),
        name="edge_backward",
    )(features, out_grad, weight, neighbour_slot, argmax_edge)


def solution(mesh):
    return jax.shard_map(
        on_device,
        mesh=mesh,
        in_specs=(P("blk", None), P("blk", "ch"), P("ch", None), P("blk", None), P("blk", "ch")),
        out_specs=(P("blk", None), P("ch", None)),
        check_vma=False,
    )
```

time: 237 us -> 55.8 us (0.24)
  starting transfers between devices: 89.4 us -> 0 us
  matrix products: 54 us -> 0 us
  Pallas kernels: 0 us -> 51.2 us
  loops' own time: 39.5 us -> 0 us
  local copies, waits for them, and re-layouts: 30.6 us -> 3.76 us
  waiting for transfers between devices: 18.6 us -> 0 us
    ppermute x16 -> x0, starting transfers between devices: 56.6 us -> none  [shifted(): return lax.ppermute(block, axis, route)]
    dot_general x45 -> x0, matrix products: 54 us -> none  [the longest x20 26.6 us: per_edge(): jnp.dot(picked, w_nbr_t, preferred_element_type=jnp.float32)]
    pallas_call x0 -> x1, Pallas kernels: none -> 51.2 us  [on_device(): pl.pallas_call(kernel, out_shape=(jax.ShapeDtypeStruct((PTS, CIN), F32),...]
    another operation x1 -> x0, loops' own time: 39.5 us -> none  [point_block(): lax.scan(per_edge, (window_acc, start_total), edge_order)]
    all_to_all x5 -> x0, starting transfers between devices: 32.8 us -> none  [the longest x3 23.3 us: from_everyone(): return lax.all_to_all(copies, axis, split_axis=0, concat_axis=0, tiled=True)]
    dynamic_slice x40 -> x0, local copies, waits for them, and re-layouts: 25.9 us -> none  [the longest x20 14.1 us: per_edge(): slot_col = lax.dynamic_slice_in_dim(slot_rows, edge_index, 1, 1)]
    all_to_all x5 -> x0, waiting for transfers between devices: 13.5 us -> none  [the longest x3 13.5 us: from_everyone(): return lax.all_to_all(copies, axis, split_axis=0, concat_axis=0, tiled=True)]
    ppermute x16 -> x0, waiting for transfers between devices: 5.09 us -> none  [shifted(): return lax.ppermute(block, axis, route)]
  transfers between devices with their start and end apart: 21 -> 0, of which waited for: 7 -> 0; matrix products, arithmetic and copies ran while one was open for 2% -> 0% of each run, Pallas kernels for 0% -> 0%
where the time goes in v1:
time: 55.8 us; the launch traced here: 55.7 us
  Pallas kernels  51.2 us (92%)
  local copies, waits for them, and re-layouts  3.76 us (7%)
  between operations  0.65 us (1%)
    pallas_call x1, Pallas kernels, on_device(): pl.pallas_call(kernel, out_shape=(jax.ShapeDtypeStruct((PTS, CIN), F32),...  51.2 us
    unnamed x5, local copies, waits for them, and re-layouts  3.76 us

profile of v1, /device:TPU:1, one launch (start us, length us, event | category | flops | bytes accessed | tf_op | source)
XLA Modules:
  0.0 55.7 jit_solution(7701560825292743378)
XLA Ops:
  0.6 1.5 %copy.7.s_hbm = s32[256,20]{1,0:T(8,128)} copy(s32[256,20]{0,1:T(8,128)} %param.8) | data formatting | bytes 40960 | tf_op args[3]
  2.1 51.2 %edge_backward.1 = (f32[256,128]{1,0:T(8,128)}, f32[128,256]{1,0:T(8,128)}) custom-call(bf16[256,128]{1,0:T(8,128)(2,1)} %f_hbm.1, bf16[256,128]{1,0:T(8,128)(2,1)} %g_hbm.1, bf16[128,256]{1,0:T(8,128)(2,1)} %w_hbm.1, s32[256,20]{1,0:T(8,128)} %copy.7.s_hbm, s32[256,128]{1,0:T(8,128)} %a_hbm.1), custom_call_target="tpu_custom_call" | custom-call | tf_op jit(solution)/shard_map/edge_backward/pallas_call | solution.py:216
  53.4 0.0 copy-start
  53.4 1.6 %copy.10 = f32[256,128]{1,0:T(8,128)} copy(f32[256,128]{1,0:T(8,128)} %get-tuple-element.4) | data formatting | bytes 262144
  55.0 0.0 copy-done
  55.0 0.7 %copy.11 = f32[128,256]{1,0:T(8,128)} copy(f32[128,256]{1,0:T(8,128)S(1)} %copy-done) | data formatting | bytes 262144
Async XLA Ops:
  53.4 1.6 %copy-start = (f32[128,256]{1,0:T(8,128)S(1)}, f32[128,256]{1,0:T(8,128)}, u32[]{:S(2)}) copy-start(f32[128,256]{1,0:T(8,128)} %get-tuple-element.5) | copy-start | bytes 393220

commit v2 on v1

v2 whole, which is shorter than its diff:
```python
import jax
import jax.numpy as jnp
from jax import lax
from jax.experimental import pallas as pl
from jax.experimental.pallas import tpu as pltpu
from jax.sharding import PartitionSpec as P

REACH = 4
SPAN = 2 * REACH + 1
NB = 128
PTS = 256
HALF = 128
CIN = 128
KNN = 20
MESH = pl.DeviceIdType.MESH
F32, BF16, I32 = jnp.float32, jnp.bfloat16, jnp.int32
NT = (((1,), (1,)), ((), ()))
TN = (((0,), (0,)), ((), ()))
PAIRS = REACH + 1
SPARE = SPAN


def silu_slope(pre):
    sig = jax.nn.sigmoid(pre)
    return sig * (1.0 + pre * (1.0 - sig))


def kernel(
    f_hbm, g_hbm, w_hbm, s_hbm, a_hbm, fgv, wgo,
    win, gv, wv, sv, av, s_t, low_t, grp_t, onehot, edges, pre, chosen, upper_s, edge_s, nbr,
    con_f, con_b, part_in, summed, got, wgv, rs_in, z_in, piece,
    in_sem, far_s, far_r, half_s, half_r, pp_s, pp_r, c_s, c_r,
    ar_s, ar_r, fo_s, fo_r,
):
    b = lax.axis_index("blk")
    c = lax.axis_index("ch")
    partner = (b, 1 - c)
    line, z = b // 8, b % 8
    x, y = line // 4, line % 4

    def along(k):
        return (lax.rem(b + k + NB, NB), c)

    def in_plane(j):
        t = j + j // 10
        q = lax.rem(x + t // 4 + 2, 4) * 4 + lax.rem(y + t % 4 + 2, 4)
        return q, (q * 8 + z, c)

    def in_line(j):
        return (line * 8 + lax.rem(z + 4 + j + j // 4, 8), c)

    bar = pltpu.get_barrier_semaphore()

    def greet(d):
        pl.semaphore_signal(bar, inc=1, device_id=d, device_id_type=MESH)

    loads = [
        pltpu.make_async_copy(f_hbm, win.at[REACH], in_sem.at[0]),
        pltpu.make_async_copy(s_hbm, sv, in_sem.at[1]),
        pltpu.make_async_copy(a_hbm, av, in_sem.at[2]),
        pltpu.make_async_copy(w_hbm, wv, in_sem.at[3]),
        pltpu.make_async_copy(g_hbm, gv, in_sem.at[4]),
    ]
    loads[0].start()

    @pl.loop(1, REACH + 1)
    def _(k):
        greet(along(k))
        greet(along(-k))

    greet(partner)
    pl.loop(0, 7)(lambda j: greet(in_line(j)))
    pl.loop(0, 15)(lambda j: greet(in_plane(j)[1]))
    for cp in loads[1:]:
        cp.start()
    loads[0].wait()
    pl.semaphore_wait(bar, 2 * REACH + 1 + 7 + 15)

    my_rows = pl.ds(pl.multiple_of(c * HALF, HALF), HALF)
    its_rows = pl.ds(pl.multiple_of((1 - c) * HALF, HALF), HALF)

    def rcopy(src, dst, ss, rs, dev):
        return pltpu.make_async_remote_copy(
            src_ref=src, dst_ref=dst, send_sem=ss, recv_sem=rs, device_id=dev, device_id_type=MESH
        )

    def far_copy(w):
        return rcopy(win.at[REACH, my_rows], win.at[w, my_rows], far_s.at[w], far_r.at[w], along(REACH - w))

    def half_copy(w):
        return rcopy(win.at[w, my_rows], win.at[w, my_rows], half_s.at[w], half_r.at[w], partner)

    def part_copy(w):
        return rcopy(con_b.at[w, its_rows], part_in.at[w], pp_s.at[w], pp_r.at[w], partner)

    def sum_copy(w):
        return rcopy(summed.at[w], got.at[8 - w], c_s.at[w], c_r.at[8 - w], along(w - REACH))

    @pl.loop(1, REACH + 1)
    def _(k):
        far_copy(REACH - k).start()
        far_copy(REACH + k).start()

    for cp in loads[1:]:
        cp.wait()
    s_t[...] = jnp.zeros_like(s_t)
    s_t[:KNN, :] = sv[...]
    idx = jnp.take_along_axis(s_t[...].T, av[...], axis=1, mode="promise_in_bounds")
    idx_t = idx.T
    low_t[...] = idx_t & 127
    grp_t[...] = idx_t >> 7

    def w_nbr():
        return wv[:, CIN:]

    def w_diff():
        return (wv[:, :CIN].astype(F32) - wv[:, CIN:].astype(F32)).astype(BF16)

    ids = [(lax.broadcasted_iota(I32, (16, PTS), 0) + 16 * j).astype(F32).astype(BF16) for j in range(8)]
    one, zero = jnp.ones((16, PTS), BF16), jnp.zeros((16, PTS), BF16)

    @pl.loop(0, KNN)
    def _(k):
        row = s_t[pl.ds(k, 1), :]
        low = (row & 127).astype(F32)
        blk = row >> 8
        cols = pl.ds(pl.multiple_of(k * PTS, PTS), PTS)
        for n in range(2 * PAIRS):
            at = n * HALF
            w = (REACH - n // 2) if n % 2 == 0 else (REACH + n // 2 if n > 1 else SPARE)
            key = jnp.broadcast_to(jnp.where(blk == w, low, -1.0), (16, PTS)).astype(BF16)
            for j in range(8):
                onehot[at + 16 * j : at + 16 * j + 16, cols] = jnp.where(ids[j] == key, one, zero)

    pre[...] = lax.dot_general(w_diff(), win[REACH], NT, preferred_element_type=F32)

    def pick(w):
        vals = lax.dot_general(w_nbr(), win[w], NT, preferred_element_type=F32)
        for h in range(2):
            cols = slice(h * HALF, (h + 1) * HALF)
            low, grp, p = low_t[:, cols], grp_t[:, cols], pre[:, cols]
            for g in range(2):
                table = vals[:, g * HALF : (g + 1) * HALF]
                hit = jnp.take_along_axis(table, low, axis=1, mode="promise_in_bounds")
                p = jnp.where(grp == 2 * w + g, p + hit, p)
            pre[:, cols] = p

    upper_s[...] = (idx >> 7) & 1
    upper = upper_s[...]
    af = av[...].astype(F32)
    chosen[...] = jnp.concatenate(
        [jnp.where(upper == 0, af, -1.0), jnp.where(upper == 1, af, -1.0)], axis=1
    ).astype(BF16)
    nbr[...] = jnp.zeros_like(nbr)
    win[SPARE] = jnp.zeros_like(win[SPARE])

    @pl.loop(0, PAIRS)
    def _(n):
        near, wide = REACH - n, jnp.where(n == 0, SPARE, REACH + n)

        def forward(k):
            for w in (REACH - k, REACH + k):
                far_copy(w).wait_recv()
                half_copy(w).start()

        @pl.when(n < REACH)
        def _():
            forward(n + 1)

        @pl.when(n > 0)
        def _():
            half_copy(near).wait_recv()
            half_copy(wide).wait_recv()

        pick(near)
        pick(wide)
        edge = (gv[...].astype(F32) * silu_slope(pre[...].T)).astype(BF16)
        edge_s[...] = edge
        ef, upper = edge.astype(F32), upper_s[...]
        e2 = jnp.concatenate([jnp.where(upper == 0, ef, 0.0), jnp.where(upper == 1, ef, 0.0)], axis=1).astype(BF16)
        a2 = chosen[...]
        for k in range(KNN):
            edges[k * PTS : (k + 1) * PTS, :] = jnp.where(a2 == jnp.asarray(k, BF16), e2, jnp.zeros_like(e2))
        rows = pl.ds(pl.multiple_of(n * PTS, PTS), PTS)
        sums = jnp.dot(onehot[rows, :], edges[...], preferred_element_type=F32).astype(BF16)
        extra = jnp.zeros((HALF, CIN), F32)
        for m, w in enumerate((near, wide)):
            ga = sums[m * HALF : (m + 1) * HALF, :]
            ga = jnp.concatenate([ga[:, :HALF], ga[:, HALF:]], axis=0)
            extra = extra + lax.dot_general(ga, win[w], TN, preferred_element_type=F32)
            con = jnp.dot(ga, w_nbr(), preferred_element_type=F32)
            con_f[w] = con
            con_b[w] = con.astype(BF16)
        nbr[...] += extra

        @pl.when(n > 0)
        def _():
            part_copy(near).start()
            part_copy(wide).start()

    edge = edge_s[...]
    own_part = lax.dot_general(edge, win[REACH], TN, preferred_element_type=F32)
    wgv[:, :CIN] = own_part
    wgv[:, CIN:] = nbr[...] - own_part

    def rows8(q):
        return pl.ds(pl.multiple_of(q * 8, 8), 8)

    @pl.loop(0, 15)
    def _(j):
        q, d = in_plane(j)
        rcopy(wgv.at[rows8(q)], rs_in.at[j], ar_s.at[0], ar_r.at[0], d).start()

    con = con_f[REACH] + jnp.dot(edge, w_diff(), preferred_element_type=F32)
    con_f[REACH] = con
    con_b[REACH] = con.astype(BF16)
    part_copy(REACH).start()

    def send_on(w):
        part_copy(w).wait_recv()
        summed[w] = (con_f[w, my_rows, :] + part_in[w].astype(F32)).astype(BF16)
        sum_copy(w).start()

    @pl.loop(1, REACH + 1)
    def _(k):
        send_on(REACH - k)
        send_on(REACH + k)

    part_copy(REACH).wait_recv()
    fgv[my_rows, :] = con_f[REACH, my_rows, :] + part_in[REACH].astype(F32)

    my_piece = rows8(line)
    rcopy(rs_in, rs_in, ar_s.at[0], ar_r.at[0], partner).wait_recv()
    piece[0] = wgv[my_piece, :] + jnp.sum(rs_in[...], axis=0)
    pl.loop(0, 7)(lambda j: rcopy(piece.at[0], z_in.at[j], ar_s.at[1], ar_r.at[1], in_line(j)).start())
    rcopy(z_in, z_in, ar_s.at[1], ar_r.at[1], partner).wait_recv()
    piece[1] = (piece[0] + jnp.sum(z_in[...], axis=0)) * (NB * PTS) ** -0.5
    pl.loop(0, 15)(
        lambda j: rcopy(piece.at[1], wgo.at[my_piece], ar_s.at[2], ar_r.at[2], in_plane(j)[1]).start()
    )
    wgo[my_piece, :] = piece[1]

    @pl.loop(1, REACH + 1)
    def _(k):
        for w in (REACH - k, REACH + k):
            rcopy(summed.at[w], got.at[w], c_s.at[w], c_r.at[w], partner).wait_recv()
            fgv[my_rows, :] += got[w].astype(F32)

    fo = rcopy(fgv.at[my_rows], fgv.at[my_rows], fo_s, fo_r, partner)
    fo.start()

    @pl.loop(1, REACH + 1)
    def _(k):
        for w in (REACH - k, REACH + k):
            far_copy(w).wait_send()
            half_copy(w).wait_send()
            part_copy(w).wait_send()
            sum_copy(w).wait_send()

    part_copy(REACH).wait_send()
    rcopy(rs_in, rs_in, ar_s.at[0], ar_r.at[0], partner).wait_send()
    rcopy(z_in, z_in, ar_s.at[1], ar_r.at[1], partner).wait_send()
    rcopy(rs_in, rs_in, ar_s.at[2], ar_r.at[2], partner).wait_send()
    rcopy(rs_in, rs_in, ar_s.at[2], ar_r.at[2], partner).wait_recv()
    rcopy(fgv.at[my_rows], fgv.at[its_rows], fo_s, fo_r, partner).wait()


def flush_kernel(fg_ref, wg_ref, fg_hbm, wg_hbm, sem):
    out_fg = pltpu.make_async_copy(fg_ref, fg_hbm, sem.at[0])
    out_wg = pltpu.make_async_copy(wg_ref, wg_hbm, sem.at[1])
    out_fg.start()
    out_wg.start()
    out_fg.wait()
    out_wg.wait()


def flush(fg, wg):
    return pl.pallas_call(
        flush_kernel,
        out_shape=(jax.ShapeDtypeStruct(fg.shape, F32), jax.ShapeDtypeStruct(wg.shape, F32)),
        in_specs=[pl.BlockSpec(memory_space=pltpu.VMEM)] * 2,
        out_specs=[pl.BlockSpec(memory_space=pl.ANY)] * 2,
        scratch_shapes=[pltpu.SemaphoreType.DMA((2,))],
        name="flush",
    )(pltpu.with_memory_space_constraint(fg, pltpu.VMEM), pltpu.with_memory_space_constraint(wg, pltpu.VMEM))


def on_device(features, out_grad, weight, neighbour_slot, argmax_edge):
    v = pltpu.VMEM
    dma = pltpu.SemaphoreType.DMA
    fg, wg = pl.pallas_call(
        kernel,
        out_shape=(v((PTS, CIN), F32), v((HALF, 2 * CIN), F32)),
        in_specs=[pl.BlockSpec(memory_space=pl.ANY)] * 5,
        out_specs=[pl.BlockSpec(memory_space=pltpu.VMEM)] * 2,
        scratch_shapes=[
            v((SPAN + 1, PTS, CIN), BF16), v((PTS, HALF), BF16), v((HALF, 2 * CIN), BF16), v((KNN, PTS), I32),
            v((PTS, HALF), I32), v((128, PTS), I32), v((HALF, PTS), I32), v((HALF, PTS), I32),
            v((2 * PAIRS * HALF, KNN * PTS), BF16), v((KNN * PTS, 2 * HALF), BF16), v((HALF, PTS), F32),
            v((PTS, 2 * HALF), BF16), v((PTS, HALF), I32), v((PTS, HALF), BF16), v((HALF, CIN), F32),
            v((SPAN + 1, PTS, CIN), F32), v((SPAN + 1, PTS, CIN), BF16), v((SPAN, HALF, CIN), BF16),
            v((SPAN, HALF, CIN), BF16), v((SPAN, HALF, CIN), BF16), v((HALF, 2 * CIN), F32),
            v((15, 8, 2 * CIN), F32), v((7, 8, 2 * CIN), F32), v((2, 8, 2 * CIN), F32),
            dma((5,)), dma((SPAN,)), dma((SPAN,)), dma((SPAN,)), dma((SPAN,)), dma((SPAN,)), dma((SPAN,)),
            dma((SPAN,)), dma((SPAN,)), dma((3,)), dma((3,)),
            dma, dma,
        ],
        compiler_params=pltpu.CompilerParams(
            collective_id=0, has_side_effects=True, vmem_limit_bytes=56 * 2**20
        ),
        name="edge_backward",
    )(features, out_grad, weight, neighbour_slot.T, argmax_edge)
    return flush(fg, wg)


def solution(mesh):
    return jax.shard_map(
        on_device,
        mesh=mesh,
        in_specs=(P("blk", None), P("blk", "ch"), P("ch", None), P("blk", None), P("blk", "ch")),
        out_specs=(P("blk", None), P("ch", None)),
        check_vma=False,
    )
```

time: 55.8 us -> 46.8 us (0.84)
  Pallas kernels: 51.2 us -> 46 us
  local copies, waits for them, and re-layouts: 3.76 us -> 0 us
    pallas_call x1 -> x2, Pallas kernels: 51.2 us -> 46 us  [the longest x1 45.3 us: on_device(): pl.pallas_call(kernel, out_shape=(v((PTS, CIN), F32), v((HALF, 2 * CIN),...]
    unnamed x5 -> x0, local copies, waits for them, and re-layouts: 3.76 us -> none
where the time goes in v2:
time: 46.8 us; the launch traced here: 46.6 us
  Pallas kernels  46 us (98%)
  between operations  0.64 us (1%)
    pallas_call x1, Pallas kernels, on_device(): pl.pallas_call(kernel, out_shape=(v((PTS, CIN), F32), v((HALF, 2 * CIN),...  45.3 us

profile of v2, /device:TPU:1, one launch (start us, length us, event | category | flops | bytes accessed | tf_op | source)
XLA Modules:
  0.0 46.6 jit_solution(5925950218176850267)
XLA Ops:
  0.6 45.3 %edge_backward.1 = (f32[256,128]{1,0:T(8,128)S(1)}, f32[128,256]{1,0:T(8,128)S(1)}) custom-call(bf16[256,128]{1,0:T(8,128)(2,1)} %f_hbm.1, bf16[256,128]{1,0:T(8,128)(2,1)} %g_hbm.1, bf16[128,256]{1,0:T(8,128)(2,1)} %w_hbm.1, s32[20,256]{1,0:T(8,128)} %bitcast.1, s32[256,128]{1,0:T(8,128)} %a_hbm.1), custom_call_target="tpu_custom_call" | custom-call | tf_op jit(solution)/shard_map/edge_backward/pallas_call | solution.py:291
  45.9 0.7 %flush.1 = (f32[256,128]{1,0:T(8,128)}, f32[128,256]{1,0:T(8,128)}) custom-call(f32[256,128]{1,0:T(8,128)S(1)} %get-tuple-element.4.fg_ref, f32[128,256]{1,0:T(8,128)S(1)} %get-tuple-element.5.wg_ref), custom_call_target="tpu_custom_call" | custom-call | tf_op jit(solution)/shard_map/flush/pallas_call | solution.py:278

commit v3 on v2

--- a/solution.py
+++ b/solution.py
@@ -28,7 +28,7 @@
 def kernel(
     f_hbm, g_hbm, w_hbm, s_hbm, a_hbm, fgv, wgo,
     win, gv, wv, sv, av, s_t, low_t, grp_t, onehot, edges, pre, chosen, upper_s, edge_s, nbr,
-    con_f, con_b, part_in, summed, got, wgv, rs_in, z_in, piece,
+    con_f, con_b, part_in, summed, got, wgv, wgb, wg_all, rs_in, z_in, piece_b,
     in_sem, far_s, far_r, half_s, half_r, pp_s, pp_r, c_s, c_r,
     ar_s, ar_r, fo_s, fo_r,
 ):
@@ -41,13 +41,12 @@
     def along(k):
         return (lax.rem(b + k + NB, NB), c)
 
-    def in_plane(j):
-        t = j + j // 10
-        q = lax.rem(x + t // 4 + 2, 4) * 4 + lax.rem(y + t % 4 + 2, 4)
-        return q, (q * 8 + z, c)
-
-    def in_line(j):
-        return (line * 8 + lax.rem(z + 4 + j + j // 4, 8), c)
+    xs = [lax.rem(x + d, 4) * 32 for d in (2, 1, 3)] + [x * 32]
+    ys = [lax.rem(y + d, 4) * 8 for d in (2, 1, 3)] + [y * 8]
+    at_plane = [(p, r) for t in range(6) for p in range(4) for r in range(4) if p + r == t]
+    plane = [xs[p] + ys[r] for p, r in at_plane]
+    across = [(q + z, c) for q in plane]
+    zline = [(line * 8 + lax.rem(z + d, 8), c) for d in (4, 3, 5, 2, 6, 1, 7)]
 
     bar = pltpu.get_barrier_semaphore()
 
@@ -63,14 +62,11 @@
     ]
     loads[0].start()
 
-    @pl.loop(1, REACH + 1)
-    def _(k):
+    for k in (4, 3, 2, 1):
         greet(along(k))
         greet(along(-k))
-
-    greet(partner)
-    pl.loop(0, 7)(lambda j: greet(in_line(j)))
-    pl.loop(0, 15)(lambda j: greet(in_plane(j)[1]))
+    for d in across + zline + [partner]:
+        greet(d)
     for cp in loads[1:]:
         cp.start()
     loads[0].wait()
@@ -154,6 +150,12 @@
     nbr[...] = jnp.zeros_like(nbr)
     win[SPARE] = jnp.zeros_like(win[SPARE])
 
+    def send_on(k):
+        for w in (REACH - k, REACH + k):
+            part_copy(w).wait_recv()
+            summed[w] = (con_f[w, my_rows, :] + part_in[w].astype(F32)).astype(BF16)
+            sum_copy(w).start()
+
     @pl.loop(0, PAIRS)
     def _(n):
         near, wide = REACH - n, jnp.where(n == 0, SPARE, REACH + n)
@@ -163,7 +165,7 @@
                 far_copy(w).wait_recv()
                 half_copy(w).start()
 
-        @pl.when(n < REACH)
+        @pl.when(n < REACH - 1)
         def _():
             forward(n + 1)
 
@@ -198,47 +200,41 @@
             part_copy(near).start()
             part_copy(wide).start()
 
+        @pl.when(n == REACH - 1)
+        def _():
+            forward(REACH)
+            pl.loop(1, REACH)(send_on)
+
     edge = edge_s[...]
     own_part = lax.dot_general(edge, win[REACH], TN, preferred_element_type=F32)
-    wgv[:, :CIN] = own_part
-    wgv[:, CIN:] = nbr[...] - own_part
-
-    def rows8(q):
-        return pl.ds(pl.multiple_of(q * 8, 8), 8)
-
-    @pl.loop(0, 15)
-    def _(j):
-        q, d = in_plane(j)
-        rcopy(wgv.at[rows8(q)], rs_in.at[j], ar_s.at[0], ar_r.at[0], d).start()
+    both = (own_part, nbr[...] - own_part)
+    for q in range(16):
+        wgv[q] = jnp.concatenate([v[q * 8 : q * 8 + 8, :] for v in both], axis=0)
+    wgb[...] = wgv[...].astype(BF16)
+
+    for j, (q, d) in enumerate(zip(plane, across)):
+        rcopy(wgb.at[q // 8], rs_in.at[j], ar_s.at[0], ar_r.at[0], d).start()
 
     con = con_f[REACH] + jnp.dot(edge, w_diff(), preferred_element_type=F32)
     con_f[REACH] = con
     con_b[REACH] = con.astype(BF16)
     part_copy(REACH).start()
 
-    def send_on(w):
-        part_copy(w).wait_recv()
-        summed[w] = (con_f[w, my_rows, :] + part_in[w].astype(F32)).astype(BF16)
-        sum_copy(w).start()
-
-    @pl.loop(1, REACH + 1)
-    def _(k):
-        send_on(REACH - k)
-        send_on(REACH + k)
-
+    send_on(REACH)
     part_copy(REACH).wait_recv()
     fgv[my_rows, :] = con_f[REACH, my_rows, :] + part_in[REACH].astype(F32)
 
-    my_piece = rows8(line)
     rcopy(rs_in, rs_in, ar_s.at[0], ar_r.at[0], partner).wait_recv()
-    piece[0] = wgv[my_piece, :] + jnp.sum(rs_in[...], axis=0)
-    pl.loop(0, 7)(lambda j: rcopy(piece.at[0], z_in.at[j], ar_s.at[1], ar_r.at[1], in_line(j)).start())
+    piece = wgv[line] + jnp.sum(rs_in[...].astype(F32), axis=0)
+    piece_b[0] = piece.astype(BF16)
+    for j, d in enumerate(zline):
+        rcopy(piece_b.at[0], z_in.at[j], ar_s.at[1], ar_r.at[1], d).start()
     rcopy(z_in, z_in, ar_s.at[1], ar_r.at[1], partner).wait_recv()
-    piece[1] = (piece[0] + jnp.sum(z_in[...], axis=0)) * (NB * PTS) ** -0.5
-    pl.loop(0, 15)(
-        lambda j: rcopy(piece.at[1], wgo.at[my_piece], ar_s.at[2], ar_r.at[2], in_plane(j)[1]).start()
-    )
-    wgo[my_piece, :] = piece[1]
+    piece = (piece + jnp.sum(z_in[...].astype(F32), axis=0)) * (NB * PTS) ** -0.5
+    piece_b[1] = piece.astype(BF16)
+    for d in across:
+        rcopy(piece_b.at[1], wg_all.at[line], ar_s.at[2], ar_r.at[2], d).start()
+    wg_all[line] = piece_b[1]
 
     @pl.loop(1, REACH + 1)
     def _(k):
@@ -262,6 +258,10 @@
     rcopy(z_in, z_in, ar_s.at[1], ar_r.at[1], partner).wait_send()
     rcopy(rs_in, rs_in, ar_s.at[2], ar_r.at[2], partner).wait_send()
     rcopy(rs_in, rs_in, ar_s.at[2], ar_r.at[2], partner).wait_recv()
+    for q in range(16):
+        whole = wg_all[q].astype(F32)
+        wgo[q * 8 : q * 8 + 8, :CIN] = whole[:8]
+        wgo[q * 8 : q * 8 + 8, CIN:] = whole[8:]
     rcopy(fgv.at[my_rows], fgv.at[its_rows], fo_s, fo_r, partner).wait()
 
 
@@ -299,8 +299,9 @@
             v((2 * PAIRS * HALF, KNN * PTS), BF16), v((KNN * PTS, 2 * HALF), BF16), v((HALF, PTS), F32),
             v((PTS, 2 * HALF), BF16), v((PTS, HALF), I32), v((PTS, HALF), BF16), v((HALF, CIN), F32),
             v((SPAN + 1, PTS, CIN), F32), v((SPAN + 1, PTS, CIN), BF16), v((SPAN, HALF, CIN), BF16),
-            v((SPAN, HALF, CIN), BF16), v((SPAN, HALF, CIN), BF16), v((HALF, 2 * CIN), F32),
-            v((15, 8, 2 * CIN), F32), v((7, 8, 2 * CIN), F32), v((2, 8, 2 * CIN), F32),
+            v((SPAN, HALF, CIN), BF16), v((SPAN, HALF, CIN), BF16), v((16, 16, CIN), F32),
+            v((16, 16, CIN), BF16), v((16, 16, CIN), BF16),
+            v((15, 16, CIN), BF16), v((7, 16, CIN), BF16), v((2, 16, CIN), BF16),
             dma((5,)), dma((SPAN,)), dma((SPAN,)), dma((SPAN,)), dma((SPAN,)), dma((SPAN,)), dma((SPAN,)),
             dma((SPAN,)), dma((SPAN,)), dma((3,)), dma((3,)),
             dma, dma,

time: 46.8 us -> 43.4 us (0.927)
  Pallas kernels: 46 us -> 42.7 us
    pallas_call x1, Pallas kernels: 45.3 us -> 42 us  [on_device(): pl.pallas_call(kernel, out_shape=(v((PTS, CIN), F32), v((HALF, 2 * CIN),...]
where the time goes in v3:
time: 43.4 us; the launch traced here: 43.3 us
  Pallas kernels  42.7 us (98%)
  between operations  0.64 us (1%)
    pallas_call x1, Pallas kernels, on_device(): pl.pallas_call(kernel, out_shape=(v((PTS, CIN), F32), v((HALF, 2 * CIN),...  42 us

profile of v3, /device:TPU:1, one launch (start us, length us, event | category | flops | bytes accessed | tf_op | source)
XLA Modules:
  0.0 43.3 jit_solution(5027319386594249248)
XLA Ops:
  0.6 42.0 %edge_backward.1 = (f32[256,128]{1,0:T(8,128)S(1)}, f32[128,256]{1,0:T(8,128)S(1)}) custom-call(bf16[256,128]{1,0:T(8,128)(2,1)} %f_hbm.1, bf16[256,128]{1,0:T(8,128)(2,1)} %g_hbm.1, bf16[128,256]{1,0:T(8,128)(2,1)} %w_hbm.1, s32[20,256]{1,0:T(8,128)} %bitcast.1, s32[256,128]{1,0:T(8,128)} %a_hbm.1), custom_call_target="tpu_custom_call" | custom-call | tf_op jit(solution)/shard_map/edge_backward/pallas_call | solution.py:291
  42.6 0.7 %flush.1 = (f32[256,128]{1,0:T(8,128)}, f32[128,256]{1,0:T(8,128)}) custom-call(f32[256,128]{1,0:T(8,128)S(1)} %get-tuple-element.4.fg_ref, f32[128,256]{1,0:T(8,128)S(1)} %get-tuple-element.5.wg_ref), custom_call_target="tpu_custom_call" | custom-call | tf_op jit(solution)/shard_map/flush/pallas_call | solution.py:278

commit v4 on v3

--- a/solution.py
+++ b/solution.py
@@ -80,11 +80,15 @@
             src_ref=src, dst_ref=dst, send_sem=ss, recv_sem=rs, device_id=dev, device_id_type=MESH
         )
 
-    def far_copy(w):
-        return rcopy(win.at[REACH, my_rows], win.at[w, my_rows], far_s.at[w], far_r.at[w], along(REACH - w))
-
-    def half_copy(w):
-        return rcopy(win.at[w, my_rows], win.at[w, my_rows], half_s.at[w], half_r.at[w], partner)
+    side = 1 - 2 * c
+
+    def far_copy(k):
+        w = REACH - side * k
+        return rcopy(win.at[REACH], win.at[w], far_s.at[k], far_r.at[k], along(side * k))
+
+    def swap_copy(k):
+        w = REACH - side * k
+        return rcopy(win.at[w], win.at[w], half_s.at[k], half_r.at[k], partner)
 
     def part_copy(w):
         return rcopy(con_b.at[w, its_rows], part_in.at[w], pp_s.at[w], pp_r.at[w], partner)
@@ -94,8 +98,7 @@
 
     @pl.loop(1, REACH + 1)
     def _(k):
-        far_copy(REACH - k).start()
-        far_copy(REACH + k).start()
+        far_copy(k).start()
 
     for cp in loads[1:]:
         cp.wait()
@@ -161,9 +164,8 @@
         near, wide = REACH - n, jnp.where(n == 0, SPARE, REACH + n)
 
         def forward(k):
-            for w in (REACH - k, REACH + k):
-                far_copy(w).wait_recv()
-                half_copy(w).start()
+            far_copy(k).wait_recv()
+            swap_copy(k).start()
 
         @pl.when(n < REACH - 1)
         def _():
@@ -171,8 +173,7 @@
 
         @pl.when(n > 0)
         def _():
-            half_copy(near).wait_recv()
-            half_copy(wide).wait_recv()
+            swap_copy(n).wait_recv()
 
         pick(near)
         pick(wide)
@@ -248,10 +249,10 @@
     @pl.loop(1, REACH + 1)
     def _(k):
         for w in (REACH - k, REACH + k):
-            far_copy(w).wait_send()
-            half_copy(w).wait_send()
             part_copy(w).wait_send()
             sum_copy(w).wait_send()
+        far_copy(k).wait_send()
+        swap_copy(k).wait_send()
 
     part_copy(REACH).wait_send()
     rcopy(rs_in, rs_in, ar_s.at[0], ar_r.at[0], partner).wait_send()

time: 43.4 us -> 43.3 us (level); the launches traced: 43.3 us -> 42.6 us
  Pallas kernels: 42.7 us -> 42 us
    pallas_call x1, Pallas kernels: 42 us -> 41.3 us  [on_device(): pl.pallas_call(kernel, out_shape=(v((PTS, CIN), F32), v((HALF, 2 * CIN),...]
where the time goes in v4:
time: 43.3 us; the launch traced here: 42.6 us
  Pallas kernels  42 us (97%)
  between operations  0.64 us (1%)
    pallas_call x1, Pallas kernels, on_device(): pl.pallas_call(kernel, out_shape=(v((PTS, CIN), F32), v((HALF, 2 * CIN),...  41.3 us

profile of v4, /device:TPU:1, one launch (start us, length us, event | category | flops | bytes accessed | tf_op | source)
XLA Modules:
  0.0 42.6 jit_solution(14220588327221495865)
XLA Ops:
  0.6 41.3 %edge_backward.1 = (f32[256,128]{1,0:T(8,128)S(1)}, f32[128,256]{1,0:T(8,128)S(1)}) custom-call(bf16[256,128]{1,0:T(8,128)(2,1)} %f_hbm.1, bf16[256,128]{1,0:T(8,128)(2,1)} %g_hbm.1, bf16[128,256]{1,0:T(8,128)(2,1)} %w_hbm.1, s32[20,256]{1,0:T(8,128)} %bitcast.1, s32[256,128]{1,0:T(8,128)} %a_hbm.1), custom_call_target="tpu_custom_call" | custom-call | tf_op jit(solution)/shard_map/edge_backward/pallas_call | solution.py:292
  41.9 0.7 %flush.1 = (f32[256,128]{1,0:T(8,128)}, f32[128,256]{1,0:T(8,128)}) custom-call(f32[256,128]{1,0:T(8,128)S(1)} %get-tuple-element.4.fg_ref, f32[128,256]{1,0:T(8,128)S(1)} %get-tuple-element.5.wg_ref), custom_call_target="tpu_custom_call" | custom-call | tf_op jit(solution)/shard_map/flush/pallas_call | solution.py:279
